TPU v7x, 32 devices: a whole 2x2x4 slice. The times are simulated.
32 devices in a mesh: chan: 16 (over z, x, core), freq: 2 (over y).
Axes of the slice: x: 2, y: 2, z: 4, core: 2. Of those that a mesh axis runs over, the one named last changes fastest.
Arguments:
- signal: bfloat16 [32, 1024, 2048], P('freq', 'chan'), may hold values from -1000 to 1000
- spatial_taps: float32 [33, 512], replicated, may hold values from -1 to 1
Outputs:
- cross_spectra: bfloat16 [512, 2, 1024, 16], P('freq', None, 'chan')
All inputs are finite; a program needn't handle non-finite values.
Results may differ from a plain program's by a relative error of at most 0.0075.
Values may be sent and summed in bfloat16 or wider, within the bound.
A program may use at most 64 MiB of HBM per device.

v0:
```python
import functools
import math

import jax
import jax.numpy as jnp
import numpy as np
from jax import lax
from jax.experimental import pallas as pl
from jax.experimental.pallas import tpu as pltpu
from jax.sharding import PartitionSpec as P

SRC_DEV = 1
LANES = 128
FINE = 32
CBLOCK = 16
FBLOCK = 8
XBLOCK = 4
SBLOCK = 16
RUN = 3


def phase_tables(samples, bins_total):
    bins = np.concatenate([np.arange(bins_total), np.ones(LANES, np.int64)])

    def pair(times):
        phase = (times[:, None] * bins[None, :] % samples) * (2.0 * np.pi / samples)
        return np.cos(phase).astype(np.float32), np.sin(phase).astype(np.float32)

    coarse = pair(np.arange(samples // FINE) * FINE)
    fine = pair(np.arange(FINE))
    return coarse + fine


def swap_matrix(outer, inner):
    rows = outer * inner
    row = lax.broadcasted_iota(jnp.int32, (rows, rows), 0)
    col = lax.broadcasted_iota(jnp.int32, (rows, rows), 1)
    wanted = (row % inner) * outer + row // inner
    return (col == wanted).astype(jnp.bfloat16)


def fill_table(cc_ref, cs_ref, fc_ref, fs_ref, table, samples, bins):
    scale = 1.0 / math.sqrt(samples)
    fine_cos = fc_ref[...]
    fine_sin = fs_ref[...]
    half = samples // 2
    lane = lax.broadcasted_iota(jnp.int32, (1, LANES), 1)
    sign = (1 - 2 * lax.rem(lane, 2)).astype(jnp.float32)

    def step(t, carry):
        coarse_cos = cc_ref[pl.ds(t, 1), :]
        coarse_sin = cs_ref[pl.ds(t, 1), :]
        cosine = coarse_cos * fine_cos - coarse_sin * fine_sin
        sine = coarse_sin * fine_cos + coarse_cos * fine_sin
        window = 0.5 * cosine[:, bins:]
        early = (0.5 - window) * scale
        late = (0.5 + window) * scale * sign
        for offset, hann in ((0, early), (half, late)):
            rows = pl.ds(pl.multiple_of(t * FINE + offset, FINE), FINE)
            for start in range(0, bins, LANES):
                table[rows, start : start + LANES] = (
                    hann * cosine[:, start : start + LANES]
                ).astype(jnp.bfloat16)
                table[rows, bins + start : bins + start + LANES] = (
                    -hann * sine[:, start : start + LANES]
                ).astype(jnp.bfloat16)
        return carry

    lax.fori_loop(0, half // FINE, step, 0)


def dft_block(first, signal, table, padded, margin):
    windows, _, samples = signal.shape
    bins = table.shape[1] // 2
    rows = signal[:, pl.ds(first, CBLOCK), :].reshape(windows * CBLOCK, samples)
    swap = swap_matrix(CBLOCK, windows)
    step = min(2 * bins, 512)
    for start in range(0, 2 * bins, step):
        spectra = jnp.dot(
            rows, table[:, start : start + step], preferred_element_type=jnp.float32
        ).astype(jnp.bfloat16)
        swapped = jnp.dot(swap, spectra, preferred_element_type=jnp.float32)
        padded[pl.ds(margin + first, CBLOCK), :, start : start + step] = swapped.astype(
            jnp.bfloat16
        ).reshape(CBLOCK, windows, step)


def filter_block(first, taps_ref, padded, filtered, power, finished):
    taps, bins = taps_ref.shape
    windows = padded.shape[1]
    groups, width = finished.shape[0], finished.shape[4]
    power[...] = jnp.zeros_like(power)

    def tile(f, carry):
        start = pl.multiple_of(f * LANES, LANES)
        lanes = pl.ds(start, LANES)
        weights = [
            jnp.broadcast_to(taps_ref[j : j + 1, lanes], (8, LANES)) for j in range(taps)
        ]
        weights = [
            jnp.concatenate([w] * (windows // 8), axis=0).astype(jnp.bfloat16) for w in weights
        ]
        for part in range(2):
            columns = pl.ds(pl.multiple_of(part * bins + start, LANES), LANES)
            total = [None] * FBLOCK
            short = [None] * FBLOCK
            for row in range(FBLOCK + taps - 1):
                value = padded[first + row, :, columns]
                for o in range(FBLOCK):
                    j = row - o
                    if 0 <= j < taps:
                        term = weights[j] * value
                        short[o] = term if j % RUN == 0 else short[o] + term
                        if j % RUN == RUN - 1 or j == taps - 1:
                            run = short[o].astype(jnp.float32)
                            total[o] = run if total[o] is None else total[o] + run
                    if row - o == taps - 1:
                        filtered[o, :, columns] = total[o]
                        power[o] += total[o] * total[o]
        return carry

    lax.fori_loop(0, bins // LANES, tile, 0)
    mean = jnp.sum(power[...], axis=2, keepdims=True) / bins
    inverse = 1.0 / jnp.sqrt(mean + 1e-06)
    for o in range(FBLOCK):
        for part in range(2):
            for group in range(groups):
                start = part * bins + group * width
                finished[group, part, first + o] = (
                    filtered[o, :, start : start + width] * inverse[o]
                ).astype(jnp.bfloat16)


def prepare_sources(sources, q_ref, qm_ref, qp_ref):
    count, groups, _, windows, width = sources.shape
    block = min(SBLOCK, count)
    swap = swap_matrix(windows, block)
    for s0 in range(0, count, block):

        def one(j, carry):
            halves = []
            for part in range(2):
                rows = sources[s0 : s0 + block, j, part].reshape(block * windows, width)
                halves.append(
                    jnp.dot(swap, rows, preferred_element_type=jnp.float32).reshape(
                        windows, block, width
                    )
                )
            q_ref[j, :, s0 : s0 + block] = halves[0]
            qm_ref[j, :, s0 : s0 + block] = halves[0] - halves[1]
            qp_ref[j, :, s0 : s0 + block] = halves[0] + halves[1]
            return carry

        lax.fori_loop(0, groups, one, 0)


def cross_block(c0, moved, out_ref, a_ref, b_ref, ab_ref, q_ref, qm_ref, qp_ref):
    groups, _, _, windows, width = moved.shape
    count = q_ref.shape[2]
    scale = 1.0 / math.sqrt(groups * windows)
    tile = min(width, LANES)
    block = min(SBLOCK, count)
    for j in range(groups):
        for c in range(XBLOCK):
            real = moved[j, 0, c0 + c].astype(jnp.float32)
            imag = moved[j, 1, c0 + c].astype(jnp.float32)
            a_ref[c, j] = real
            b_ref[c, j] = imag
            ab_ref[c, j] = real + imag
    for s0 in range(0, count, block):
        for start in range(0, width, tile):
            lanes = slice(start, start + tile)

            def windows_of(j, total):
                total = list(total)
                for w in range(windows):
                    q = q_ref[j, w, s0 : s0 + block, lanes]
                    qm = qm_ref[j, w, s0 : s0 + block, lanes]
                    qp = qp_ref[j, w, s0 : s0 + block, lanes]
                    for c in range(XBLOCK):
                        total[3 * c] += ab_ref[c, j, w : w + 1, lanes] * q
                        total[3 * c + 1] += b_ref[c, j, w : w + 1, lanes] * qm
                        total[3 * c + 2] += a_ref[c, j, w : w + 1, lanes] * qp
                return tuple(total)

            zero = jnp.zeros((block, tile), jnp.float32)
            total = lax.fori_loop(0, groups, windows_of, (zero,) * (3 * XBLOCK))
            for c in range(XBLOCK):
                common, second, third = total[3 * c : 3 * c + 3]
                out_ref[0, c0 + c, s0 : s0 + block, lanes] = (
                    (common - second) * scale
                ).astype(jnp.bfloat16)
                out_ref[1, c0 + c, s0 : s0 + block, lanes] = (
                    (common - third) * scale
                ).astype(jnp.bfloat16)


def kernel(
    groups, count, signal_hbm, cc_ref, cs_ref, fc_ref, fs_ref, taps_ref, out_ref,
    signal, table, padded, filtered, power, finished, moved, sources, local,
    a_ref, b_ref, ab_ref, q_ref, qm_ref, qp_ref,
    load_sems, halo_send, halo_recv, y_send, y_recv, own_sems, source_own,
    source_send, source_recv, pair_send, pair_recv, first_send, first_recv,
):
    channels, samples = signal.shape[1:]
    taps, bins = taps_ref.shape
    margin = taps // 2
    half = count // 2
    blocks = channels // CBLOCK
    chunks = channels // FBLOCK
    low_end = margin // FBLOCK
    high_start = chunks - low_end
    chan = lax.axis_index("chan")
    freq = lax.axis_index("freq")
    right = lax.rem(chan + 1, count)
    left = lax.rem(chan + count - 1, count)
    partner = chan + 1 - 2 * lax.rem(chan, 2)

    def to_chan(index):
        return {"chan": index}

    loads = []
    for i in range(blocks):
        span = pl.ds(((i + blocks - 1) % blocks) * CBLOCK, CBLOCK)
        loads.append(
            pltpu.make_async_copy(
                signal_hbm.at[:, span, :], signal.at[:, span, :], load_sems.at[i]
            )
        )
        loads[-1].start()

    barrier = pltpu.get_barrier_semaphore()

    def greet(device):
        pl.semaphore_signal(
            barrier, inc=1, device_id=device, device_id_type=pl.DeviceIdType.MESH
        )

    for device in (left, right, partner):
        greet(to_chan(device))
    for d in range(1, half):
        greet(to_chan(lax.rem(chan + 2 * d, count)))
    for d in range(1, groups):
        greet({"freq": lax.rem(freq + d, groups)})

    fill_table(cc_ref, cs_ref, fc_ref, fs_ref, table, samples, bins)
    pl.semaphore_wait(barrier, 3 + half - 1 + groups - 1)

    def remote(src, dst, send, recv, device):
        return pltpu.make_async_remote_copy(
            src_ref=src, dst_ref=dst, send_sem=send, recv_sem=recv,
            device_id=device, device_id_type=pl.DeviceIdType.MESH,
        )

    low_copy = remote(
        padded.at[pl.ds(channels, margin)], padded.at[pl.ds(0, margin)],
        halo_send.at[0], halo_recv.at[0], to_chan(right),
    )
    high_copy = remote(
        padded.at[pl.ds(margin, margin)], padded.at[pl.ds(margin + channels, margin)],
        halo_send.at[1], halo_recv.at[1], to_chan(left),
    )

    def dft_step(i, carry):
        first = pl.multiple_of(lax.rem(i + blocks - 1, blocks) * CBLOCK, CBLOCK)
        span = pl.ds(first, CBLOCK)
        pltpu.make_async_copy(
            signal_hbm.at[:, span, :], signal.at[:, span, :], load_sems.at[i]
        ).wait()
        dft_block(first, signal, table, padded, margin)

        @pl.when(i == 0)
        def _():
            low_copy.start()

        @pl.when(i == blocks - 1)
        def _():
            high_copy.start()

        return carry

    lax.fori_loop(0, blocks, dft_step, 0)

    def own_copy(k):
        span = pl.ds(k * FBLOCK, FBLOCK)
        return pltpu.make_async_copy(
            finished.at[freq, :, span], moved.at[freq, :, span], own_sems.at[k]
        )

    def y_copy(k, d):
        span = pl.ds(k * FBLOCK, FBLOCK)
        target = lax.rem(freq + d, groups)
        return remote(
            finished.at[target, :, span], moved.at[freq, :, span],
            y_send.at[d - 1, k], y_recv.at[d - 1, k], {"freq": target},
        )

    def compute(k):
        filter_block(k * FBLOCK, taps_ref, padded, filtered, power, finished)

    def send(k):
        for d in range(1, groups):
            y_copy(k, d).start()
        own_copy(k).start()

    def filter_step(k, carry):
        compute(k)
        send(k)
        return carry

    def arrived(k):
        own_copy(k).wait()
        for d in range(1, groups):
            y_copy(k, d).wait_recv()

    def first_copy(d):
        target = lax.rem(freq + d, groups)
        return remote(
            finished.at[target, :, 0], local.at[freq],
            first_send.at[d - 1], first_recv.at[d - 1], {"freq": target},
        )

    ahead = low_end + max(min(3, high_start - low_end), 1)

    def early_step(k, carry):
        compute(k)

        @pl.when(k < ahead - 1)
        def _():
            send(k)

        return carry

    lax.fori_loop(low_end, ahead, early_step, 0)
    low_copy.wait_recv()
    compute(0)
    for d in range(1, groups):
        first_copy(d).start()
    own_first = pltpu.make_async_copy(finished.at[freq, :, 0], local.at[freq], source_own.at[1])
    own_first.start()
    send(ahead - 1)
    send(0)
    lax.fori_loop(ahead, high_start, filter_step, 0)
    own_first.wait()
    for d in range(1, groups):
        first_copy(d).wait_recv()

    mine = local

    def source_copy(d):
        return remote(
            mine, sources.at[chan], source_send.at[d], source_recv.at[d],
            to_chan(lax.rem(chan + 2 * d, count)),
        )

    def pair_copy(d):
        origin = lax.rem(chan + count - 2 * d, count)
        return remote(
            mine if d == 0 else sources.at[origin], sources.at[origin],
            pair_send.at[d], pair_recv.at[d], to_chan(partner),
        )

    for d in range(1, half):
        source_copy(d).start()
    pair_copy(0).start()
    keep = pltpu.make_async_copy(mine, sources.at[chan], source_own.at[0])
    keep.start()

    lax.fori_loop(1, low_end, filter_step, 0)
    high_copy.wait_recv()
    lax.fori_loop(high_start, chunks, filter_step, 0)

    for d in range(1, half):
        source_copy(d).wait_recv()
        pair_copy(d).start()
    keep.wait()
    for d in range(half):
        pair_copy(d).wait_recv()
    prepare_sources(sources, q_ref, qm_ref, qp_ref)

    def cross_step(k, carry):
        arrived(k)

        def inner(i, carry):
            cross_block(
                k * FBLOCK + i * XBLOCK, moved, out_ref,
                a_ref, b_ref, ab_ref, q_ref, qm_ref, qp_ref,
            )
            return carry

        return lax.fori_loop(0, FBLOCK // XBLOCK, inner, carry)

    lax.fori_loop(0, chunks, cross_step, 0)

    low_copy.wait_send()
    high_copy.wait_send()
    for d in range(1, groups):
        first_copy(d).wait_send()
    for d in range(1, half):
        source_copy(d).wait_send()
    for d in range(half):
        pair_copy(d).wait_send()

    def drain(k, carry):
        for d in range(1, groups):
            y_copy(k, d).wait_send()
        return carry

    lax.fori_loop(0, chunks, drain, 0)


def on_device(signal, spatial_taps):
    windows, channels, samples = signal.shape
    taps, bins = spatial_taps.shape
    margin = taps // 2
    groups = lax.axis_size("freq")
    count = lax.axis_size("chan") * SRC_DEV
    width = bins // groups
    chunks = channels // FBLOCK
    tables = [jnp.asarray(t) for t in phase_tables(samples, bins)]
    vmem = pl.BlockSpec(memory_space=pltpu.VMEM)
    dma = pltpu.SemaphoreType.DMA
    rows = pltpu.VMEM((XBLOCK, groups, windows, width), jnp.float32)
    source = pltpu.VMEM((groups, windows, count, width), jnp.float32)
    spectra = pltpu.VMEM((groups, 2, channels, windows, width), jnp.bfloat16)
    result = pl.pallas_call(
        functools.partial(kernel, groups, count),
        in_specs=[pl.BlockSpec(memory_space=pl.ANY)] + [vmem] * 5,
        out_specs=vmem,
        out_shape=jax.ShapeDtypeStruct((2, channels, count, width), jnp.bfloat16),
        scratch_shapes=[
            pltpu.VMEM(signal.shape, jnp.bfloat16),
            pltpu.VMEM((samples, 2 * bins), jnp.bfloat16),
            pltpu.VMEM((channels + 2 * margin, windows, 2 * bins), jnp.bfloat16),
            pltpu.VMEM((FBLOCK, windows, 2 * bins), jnp.float32),
            pltpu.VMEM((FBLOCK, windows, LANES), jnp.float32),
            spectra,
            spectra,
            pltpu.VMEM((count, groups, 2, windows, width), jnp.bfloat16),
            pltpu.VMEM((groups, 2, windows, width), jnp.bfloat16),
        ]
        + [rows] * 3
        + [source] * 3
        + [
            dma((channels // CBLOCK,)),
            dma((2,)),
            dma((2,)),
            dma((max(groups - 1, 1), chunks)),
            dma((max(groups - 1, 1), chunks)),
            dma((chunks,)),
            dma((2,)),
            dma((count // 2,)),
            dma((count // 2,)),
            dma((count // 2,)),
            dma((count // 2,)),
            dma((max(groups - 1, 1),)),
            dma((max(groups - 1, 1),)),
        ],
        compiler_params=pltpu.CompilerParams(
            collective_id=0, has_side_effects=True, vmem_limit_bytes=60 * 2**20
        ),
    )(signal, *tables, spatial_taps)
    return result.transpose(3, 0, 1, 2)


def solution(mesh):
    placed = (P("freq", "chan", None), P())
    return jax.shard_map(
        on_device,
        mesh=mesh,
        in_specs=placed,
        out_specs=P("freq", None, "chan", None),
        check_vma=False,
    )
```

profile of v0, /device:TPU:0, one launch (start us, length us, event | category | flops | bytes accessed | tf_op | source)
XLA Modules:
  0.0 46.0 jit_solution(9941346485514760630)
XLA Ops:
  0.0 43.7 %shard_map.64 = bf16[2,64,16,256]{3,2,1,0:T(8,128)(2,1)} custom-call(bf16[16,64,2048]{2,1,0:T(8,128)(2,1)} %signal_hbm.1, f32[64,640]{1,0:T(8,128)} %constant.8.clone.cc_ref, f32[64,640]{1,0:T(8,128)} %constant.9.clone.cs_ref, f32[32,640]{1,0:T(8,128)} %constant.10.clone.fc_ref, f32[32,640]{1,0:T(8,128)} %constant.11.clone.fs_ref, f32[33,512]{1,0:T(8,128)} %taps_ref.1), custom_call_target="tpu_custom_call" | custom-call | tf_op jit(solution)/shard_map/pallas_call | solution.py:426
  43.8 2.3 %copy.8 = bf16[256,2,64,16]{0,3,2,1:T(8,128)(2,1)} copy(bf16[256,2,64,16]{0,3,2,1:T(8,128)(2,1)} %bitcast.1) | data formatting | bytes 2097152
where the time goes:
time: 46.2 us; the launch traced here: 46 us
  Pallas kernels  43.7 us (95%)
  local copies, waits for them, and re-layouts  2.26 us (5%)
    pallas_call x1, Pallas kernels, on_device(): pl.pallas_call(functools.partial(kernel, groups, count), in_specs=[pl.Blo...  43.7 us
    unnamed x1, local copies, waits for them, and re-layouts  2.26 us

commit v1 on v0

--- a/solution.py
+++ b/solution.py
@@ -427,7 +427,7 @@
         functools.partial(kernel, groups, count),
         in_specs=[pl.BlockSpec(memory_space=pl.ANY)] + [vmem] * 5,
         out_specs=vmem,
-        out_shape=jax.ShapeDtypeStruct((2, channels, count, width), jnp.bfloat16),
+        out_shape=pltpu.VMEM((2, channels, count, width), jnp.bfloat16),
         scratch_shapes=[
             pltpu.VMEM(signal.shape, jnp.bfloat16),
             pltpu.VMEM((samples, 2 * bins), jnp.bfloat16),

time: 46.2 us -> 43.9 us (0.950)
  local copies, waits for them, and re-layouts: 2.26 us -> 0.97 us
  Pallas kernels: 43.7 us -> 42.7 us
    unnamed x1, local copies, waits for them, and re-layouts: 2.26 us -> 0.97 us
    pallas_call x1, Pallas kernels: 43.7 us -> 42.7 us  [on_device(): pl.pallas_call(functools.partial(kernel, groups, count), in_specs=[pl.Blo...]
where the time goes in v1:
time: 43.9 us; the launch traced here: 43.7 us
  Pallas kernels  42.7 us (97%)
  local copies, waits for them, and re-layouts  0.97 us (2%)
    pallas_call x1, Pallas kernels, on_device(): pl.pallas_call(functools.partial(kernel, groups, count), in_specs=[pl.Blo...  42.7 us
    unnamed x1, local copies, waits for them, and re-layouts  0.97 us

profile of v1, /device:TPU:0, one launch (start us, length us, event | category | flops | bytes accessed | tf_op | source)
XLA Modules:
  0.0 43.7 jit_solution(17132616957335248024)
XLA Ops:
  0.0 42.7 %shard_map.64 = bf16[2,64,16,256]{3,2,1,0:T(8,128)(2,1)S(1)} custom-call(bf16[16,64,2048]{2,1,0:T(8,128)(2,1)} %signal_hbm.1, f32[64,640]{1,0:T(8,128)} %constant.8.clone.cc_ref, f32[64,640]{1,0:T(8,128)} %constant.9.clone.cs_ref, f32[32,640]{1,0:T(8,128)} %constant.10.clone.fc_ref, f32[32,640]{1,0:T(8,128)} %constant.11.clone.fs_ref, f32[33,512]{1,0:T(8,128)} %taps_ref.1), custom_call_target="tpu_custom_call" | custom-call | tf_op jit(solution)/shard_map/pallas_call | solution.py:426
  42.8 1.0 %copy.8 = bf16[256,2,64,16]{0,3,2,1:T(8,128)(2,1)} copy(bf16[256,2,64,16]{0,3,2,1:T(8,128)(2,1)S(1)} %bitcast.1) | data formatting | bytes 2097152

commit v2 on v1

--- a/solution.py
+++ b/solution.py
@@ -17,6 +17,7 @@
 XBLOCK = 4
 SBLOCK = 16
 RUN = 3
+PLANE = 4
 
 
 def phase_tables(samples, bins_total):
@@ -201,6 +202,7 @@
     a_ref, b_ref, ab_ref, q_ref, qm_ref, qp_ref,
     load_sems, halo_send, halo_recv, y_send, y_recv, own_sems, source_own,
     source_send, source_recv, pair_send, pair_recv, first_send, first_recv,
+    up_sem, down_sem,
 ):
     channels, samples = signal.shape[1:]
     taps, bins = taps_ref.shape
@@ -236,15 +238,51 @@
             barrier, inc=1, device_id=device, device_id_type=pl.DeviceIdType.MESH
         )
 
-    for device in (left, right, partner):
-        greet(to_chan(device))
-    for d in range(1, half):
-        greet(to_chan(lax.rem(chan + 2 * d, count)))
+    place = lax.rem(chan, PLANE)
+    level = chan // PLANE
+    levels = count // PLANE
+
+    def when(condition, body):
+        pl.when(condition)(body)
+
+    for d in range(1, PLANE):
+        greet(to_chan(chan - place + lax.rem(place + d, PLANE)))
     for d in range(1, groups):
         greet({"freq": lax.rem(freq + d, groups)})
+    above = level < levels - 1
+    below = level > 0
+    crossing_up = jnp.logical_and(above, place == PLANE - 1)
+    crossing_down = jnp.logical_and(below, place == 0)
+    when(above, lambda: greet(to_chan(chan + PLANE)))
+    when(below, lambda: greet(to_chan(chan - PLANE)))
+    when(crossing_up, lambda: greet(to_chan(chan + 1)))
+    when(crossing_down, lambda: greet(to_chan(chan - 1)))
+    near = PLANE - 1 + groups - 1
+    for condition in (above, below, crossing_up, crossing_down):
+        near = near + condition.astype(jnp.int32)
+
+    def tell(sem, device):
+        pl.semaphore_signal(
+            sem, inc=1, device_id=to_chan(device), device_id_type=pl.DeviceIdType.MESH
+        )
+
+    def relay(i):
+        def up():
+            pl.semaphore_wait(up_sem, 1)
+            when(above, lambda: tell(up_sem, chan + PLANE))
+
+        def down():
+            pl.semaphore_wait(down_sem, 1)
+            when(below, lambda: tell(down_sem, chan - PLANE))
+
+        when(jnp.logical_and(below, i == 0), up)
+        turn = jnp.minimum(levels - 2 - level, blocks - 2)
+        when(jnp.logical_and(above, i == turn), down)
 
     fill_table(cc_ref, cs_ref, fc_ref, fs_ref, table, samples, bins)
-    pl.semaphore_wait(barrier, 3 + half - 1 + groups - 1)
+    pl.semaphore_wait(barrier, near)
+    when(jnp.logical_not(below), lambda: when(above, lambda: tell(up_sem, chan + PLANE)))
+    when(jnp.logical_not(above), lambda: when(below, lambda: tell(down_sem, chan - PLANE)))
 
     def remote(src, dst, send, recv, device):
         return pltpu.make_async_remote_copy(
@@ -268,6 +306,7 @@
             signal_hbm.at[:, span, :], signal.at[:, span, :], load_sems.at[i]
         ).wait()
         dft_block(first, signal, table, padded, margin)
+        relay(i)
 
         @pl.when(i == 0)
         def _():
@@ -455,6 +494,8 @@
             dma((count // 2,)),
             dma((max(groups - 1, 1),)),
             dma((max(groups - 1, 1),)),
+            pltpu.SemaphoreType.REGULAR,
+            pltpu.SemaphoreType.REGULAR,
         ],
         compiler_params=pltpu.CompilerParams(
             collective_id=0, has_side_effects=True, vmem_limit_bytes=60 * 2**20

time: 43.9 us -> 41.9 us (0.954)
  Pallas kernels: 42.7 us -> 40.7 us
    pallas_call x1, Pallas kernels: 42.7 us -> 40.7 us  [on_device(): pl.pallas_call(functools.partial(kernel, groups, count), in_specs=[pl.Blo...]
where the time goes in v2:
time: 41.9 us; the launch traced here: 41.7 us
  Pallas kernels  40.7 us (97%)
  local copies, waits for them, and re-layouts  0.97 us (2%)
    pallas_call x1, Pallas kernels, on_device(): pl.pallas_call(functools.partial(kernel, groups, count), in_specs=[pl.Blo...  40.7 us
    unnamed x1, local copies, waits for them, and re-layouts  0.97 us

profile of v2, /device:TPU:0, one launch (start us, length us, event | category | flops | bytes accessed | tf_op | source)
XLA Modules:
  0.0 41.7 jit_solution(14678244195873146438)
XLA Ops:
  0.0 40.7 %shard_map.64 = bf16[2,64,16,256]{3,2,1,0:T(8,128)(2,1)S(1)} custom-call(bf16[16,64,2048]{2,1,0:T(8,128)(2,1)} %signal_hbm.1, f32[64,640]{1,0:T(8,128)} %constant.8.clone.cc_ref, f32[64,640]{1,0:T(8,128)} %constant.9.clone.cs_ref, f32[32,640]{1,0:T(8,128)} %constant.10.clone.fc_ref, f32[32,640]{1,0:T(8,128)} %constant.11.clone.fs_ref, f32[33,512]{1,0:T(8,128)} %taps_ref.1), custom_call_target="tpu_custom_call" | custom-call | tf_op jit(solution)/shard_map/pallas_call | solution.py:465
  40.8 1.0 %copy.8 = bf16[256,2,64,16]{0,3,2,1:T(8,128)(2,1)} copy(bf16[256,2,64,16]{0,3,2,1:T(8,128)(2,1)S(1)} %bitcast.1) | data formatting | bytes 2097152

commit v3 on v2

--- a/solution.py
+++ b/solution.py
@@ -223,7 +223,7 @@
 
     loads = []
     for i in range(blocks):
-        span = pl.ds(((i + blocks - 1) % blocks) * CBLOCK, CBLOCK)
+        span = pl.ds((blocks - 1 - i) * CBLOCK, CBLOCK)
         loads.append(
             pltpu.make_async_copy(
                 signal_hbm.at[:, span, :], signal.at[:, span, :], load_sems.at[i]
@@ -273,11 +273,11 @@
 
         def down():
             pl.semaphore_wait(down_sem, 1)
-            when(below, lambda: tell(down_sem, chan - PLANE))
+            tell(down_sem, chan - PLANE)
 
         when(jnp.logical_and(below, i == 0), up)
         turn = jnp.minimum(levels - 2 - level, blocks - 2)
-        when(jnp.logical_and(above, i == turn), down)
+        when(jnp.logical_and(jnp.logical_and(above, below), i == turn), down)
 
     fill_table(cc_ref, cs_ref, fc_ref, fs_ref, table, samples, bins)
     pl.semaphore_wait(barrier, near)
@@ -299,27 +299,6 @@
         halo_send.at[1], halo_recv.at[1], to_chan(left),
     )
 
-    def dft_step(i, carry):
-        first = pl.multiple_of(lax.rem(i + blocks - 1, blocks) * CBLOCK, CBLOCK)
-        span = pl.ds(first, CBLOCK)
-        pltpu.make_async_copy(
-            signal_hbm.at[:, span, :], signal.at[:, span, :], load_sems.at[i]
-        ).wait()
-        dft_block(first, signal, table, padded, margin)
-        relay(i)
-
-        @pl.when(i == 0)
-        def _():
-            low_copy.start()
-
-        @pl.when(i == blocks - 1)
-        def _():
-            high_copy.start()
-
-        return carry
-
-    lax.fori_loop(0, blocks, dft_step, 0)
-
     def own_copy(k):
         span = pl.ds(k * FBLOCK, FBLOCK)
         return pltpu.make_async_copy(
@@ -359,27 +338,51 @@
             first_send.at[d - 1], first_recv.at[d - 1], {"freq": target},
         )
 
-    ahead = low_end + max(min(3, high_start - low_end), 1)
-
-    def early_step(k, carry):
-        compute(k)
-
-        @pl.when(k < ahead - 1)
+    lead = (CBLOCK + margin) // FBLOCK
+
+    def dft_step(i, carry):
+        first = pl.multiple_of((blocks - 1 - i) * CBLOCK, CBLOCK)
+        span = pl.ds(first, CBLOCK)
+
+        @pl.when(i == blocks - 1)
         def _():
-            send(k)
+            compute(lead)
+            send(lead)
+
+        pltpu.make_async_copy(
+            signal_hbm.at[:, span, :], signal.at[:, span, :], load_sems.at[i]
+        ).wait()
+        dft_block(first, signal, table, padded, margin)
+        relay(i)
+
+        @pl.when(i == 0)
+        def _():
+            low_copy.start()
+
+        @pl.when(jnp.logical_and(i == blocks - 1, chan != 0))
+        def _():
+            high_copy.start()
 
         return carry
 
-    lax.fori_loop(low_end, ahead, early_step, 0)
+    lax.fori_loop(0, blocks, dft_step, 0)
+    lax.fori_loop(lead + 1, high_start, filter_step, 0)
+    compute(low_end)
+    when(jnp.logical_and(above, level == 0), lambda: pl.semaphore_wait(down_sem, 1))
+
+    @pl.when(chan == 0)
+    def _():
+        high_copy.start()
+
     low_copy.wait_recv()
     compute(0)
     for d in range(1, groups):
         first_copy(d).start()
     own_first = pltpu.make_async_copy(finished.at[freq, :, 0], local.at[freq], source_own.at[1])
     own_first.start()
-    send(ahead - 1)
+    send(low_end)
     send(0)
-    lax.fori_loop(ahead, high_start, filter_step, 0)
+    lax.fori_loop(low_end + 1, lead, filter_step, 0)
     own_first.wait()
     for d in range(1, groups):
         first_copy(d).wait_recv()

time: 41.9 us -> 40.5 us (0.967)
  Pallas kernels: 40.7 us -> 39.3 us
    pallas_call x1, Pallas kernels: 40.7 us -> 39.3 us  [on_device(): pl.pallas_call(functools.partial(kernel, groups, count), in_specs=[pl.Blo...]
where the time goes in v3:
time: 40.5 us; the launch traced here: 40.3 us
  Pallas kernels  39.3 us (97%)
  local copies, waits for them, and re-layouts  0.97 us (2%)
    pallas_call x1, Pallas kernels, on_device(): pl.pallas_call(functools.partial(kernel, groups, count), in_specs=[pl.Blo...  39.3 us
    unnamed x1, local copies, waits for them, and re-layouts  0.97 us

profile of v3, /device:TPU:0, one launch (start us, length us, event | category | flops | bytes accessed | tf_op | source)
XLA Modules:
  0.0 40.3 jit_solution(3247344400704685026)
XLA Ops:
  0.0 39.3 %shard_map.64 = bf16[2,64,16,256]{3,2,1,0:T(8,128)(2,1)S(1)} custom-call(bf16[16,64,2048]{2,1,0:T(8,128)(2,1)} %signal_hbm.1, f32[64,640]{1,0:T(8,128)} %constant.8.clone.cc_ref, f32[64,640]{1,0:T(8,128)} %constant.9.clone.cs_ref, f32[32,640]{1,0:T(8,128)} %constant.10.clone.fc_ref, f32[32,640]{1,0:T(8,128)} %constant.11.clone.fs_ref, f32[33,512]{1,0:T(8,128)} %taps_ref.1), custom_call_target="tpu_custom_call" | custom-call | tf_op jit(solution)/shard_map/pallas_call | solution.py:468
  39.3 1.0 %copy.8 = bf16[256,2,64,16]{0,3,2,1:T(8,128)(2,1)} copy(bf16[256,2,64,16]{0,3,2,1:T(8,128)(2,1)S(1)} %bitcast.1) | data formatting | bytes 2097152

commit v4 on v3

--- a/solution.py
+++ b/solution.py
@@ -374,15 +374,19 @@
     def _():
         high_copy.start()
 
+    wrapped = chan == 0
+    split = jnp.where(wrapped, lead, low_end + 1)
+    when(wrapped, lambda: send(low_end))
+    lax.fori_loop(low_end + 1, split, filter_step, 0)
     low_copy.wait_recv()
     compute(0)
     for d in range(1, groups):
         first_copy(d).start()
     own_first = pltpu.make_async_copy(finished.at[freq, :, 0], local.at[freq], source_own.at[1])
     own_first.start()
-    send(low_end)
+    when(jnp.logical_not(wrapped), lambda: send(low_end))
     send(0)
-    lax.fori_loop(low_end + 1, lead, filter_step, 0)
+    lax.fori_loop(split, lead, filter_step, 0)
     own_first.wait()
     for d in range(1, groups):
         first_copy(d).wait_recv()

time: 40.5 us -> 39.7 us (0.980)
  Pallas kernels: 39.3 us -> 38.5 us
    pallas_call x1, Pallas kernels: 39.3 us -> 38.5 us  [on_device(): pl.pallas_call(functools.partial(kernel, groups, count), in_specs=[pl.Blo...]
where the time goes in v4:
time: 39.7 us; the launch traced here: 39.5 us
  Pallas kernels  38.5 us (97%)
  local copies, waits for them, and re-layouts  0.97 us (2%)
    pallas_call x1, Pallas kernels, on_device(): pl.pallas_call(functools.partial(kernel, groups, count), in_specs=[pl.Blo...  38.5 us
    unnamed x1, local copies, waits for them, and re-layouts  0.97 us

profile of v4, /device:TPU:0, one launch (start us, length us, event | category | flops | bytes accessed | tf_op | source)
XLA Modules:
  0.0 39.5 jit_solution(12368101089266467619)
XLA Ops:
  0.0 38.5 %shard_map.64 = bf16[2,64,16,256]{3,2,1,0:T(8,128)(2,1)S(1)} custom-call(bf16[16,64,2048]{2,1,0:T(8,128)(2,1)} %signal_hbm.1, f32[64,640]{1,0:T(8,128)} %constant.8.clone.cc_ref, f32[64,640]{1,0:T(8,128)} %constant.9.clone.cs_ref, f32[32,640]{1,0:T(8,128)} %constant.10.clone.fc_ref, f32[32,640]{1,0:T(8,128)} %constant.11.clone.fs_ref, f32[33,512]{1,0:T(8,128)} %taps_ref.1), custom_call_target="tpu_custom_call" | custom-call | tf_op jit(solution)/shard_map/pallas_call | solution.py:472
  38.5 1.0 %copy.8 = bf16[256,2,64,16]{0,3,2,1:T(8,128)(2,1)} copy(bf16[256,2,64,16]{0,3,2,1:T(8,128)(2,1)S(1)} %bitcast.1) | data formatting | bytes 2097152
